TPU v7x, 32 devices: a whole 2x2x4 slice. The times are simulated.
32 devices in a mesh: section: 8 (over z, core), ctx: 4 (over y, x).
Axes of the slice: x: 2, y: 2, z: 4, core: 2. Of those that a mesh axis runs over, the one named last changes fastest.
Arguments:
- gate_q: bfloat16 [8, 512, 4096], P('section', 'ctx'), may hold values from -6 to 6
- gate_k: bfloat16 [8, 512, 4096], P('section', 'ctx'), may hold values from -6 to 6
- value_in: bfloat16 [8, 512, 4096], P('section', 'ctx'), may hold values from -6 to 6
- filter_raw: bfloat16 [8, 512, 4096], P('section', 'ctx'), may hold values from -0.5 to 0.5
- decay_rate: float32 [8, 4096], P('section'), may hold values from 0.25 to 16
- skip_gain: float32 [8, 4096], P('section'), may hold values from -4 to 4
- grad_out: bfloat16 [8, 512, 4096], P('section', 'ctx'), may hold values from -6 to 6
Outputs:
- grad_q: bfloat16 [8, 512, 4096], P('section', 'ctx')
- grad_k: bfloat16 [8, 512, 4096], P('section', 'ctx')
- grad_passed: bfloat16 [8, 512, 4096], P('section', 'ctx')
- filter_grad: bfloat16 [8, 512, 4096], P('section', 'ctx')
- rate_grad: float32 [8, 4096], P('section')
- skip_grad: float32 [8, 4096], P('section')
All inputs are finite; a program needn't handle non-finite values.
Results may differ from a plain program's by a relative error of at most 0.013.
Values may be sent and summed in bfloat16 or wider, within the bound.
A program may use at most 128 MiB of HBM per device.

v0:
```python
import math
import jax
import jax.numpy as jnp
from jax import lax
from jax.sharding import PartitionSpec as P

exact_mode = lax.Precision.HIGHEST


def shifted(x, axis, by):
    size = lax.axis_size(axis)
    pairs = [(i, i + by) for i in range(size) if 0 <= i + by < size]
    return lax.ppermute(x, axis, pairs)


def every_table(parts_count):
    twice = 2 * parts_count
    m_index = jnp.arange(parts_count, dtype=jnp.int32)[:, None, None]
    bin_grid = jnp.arange(twice, dtype=jnp.int32).reshape(parts_count, 2).T[None]
    angle = (m_index * bin_grid % twice).astype(jnp.float32) * (math.pi / parts_count)
    return jnp.stack([jnp.cos(angle), -jnp.sin(angle)], axis=2)


def combined_tables(slot_bins, tok_rows, fft_length):
    factor_len = fft_length // tok_rows
    row_index = jnp.arange(tok_rows, dtype=jnp.int32)
    frequency = slot_bins[:, None] + factor_len * row_index[None, :]
    product = row_index[None, :, None] * frequency[:, None, :] % fft_length
    angle = product.astype(jnp.float32) * (2.0 * math.pi / fft_length)
    cosine = jnp.cos(angle)
    sine = jnp.sin(angle)
    forward_table = jnp.stack(
        [jnp.stack([cosine, -sine], axis=2), jnp.stack([sine, cosine], axis=2)], axis=1
    )
    cos_back = jnp.transpose(cosine, (0, 2, 1))
    sin_back = jnp.transpose(sine, (0, 2, 1))
    inverse_table = jnp.stack(
        [jnp.stack([cos_back, sin_back], axis=2), jnp.stack([-sin_back, cos_back], axis=2)], axis=1
    )
    return (forward_table, inverse_table)


def spectral_middle(stack_mixed, stack_filter, stack_pulled, slot_bins, tok_rows, fft_length):
    forward_table, inverse_table = combined_tables(slot_bins, tok_rows, fft_length)

    def forward(stacked):
        return jnp.einsum(
            "spjc,spjqb->sqbc", stacked.astype(jnp.float32), forward_table, precision=exact_mode
        )

    def inverse(real_part, imag_part):
        stacked = jnp.stack([real_part, imag_part], axis=1)
        return jnp.einsum("sqbc,sqbpj->spjc", stacked, inverse_table, precision=exact_mode).astype(
            jnp.bfloat16
        )

    spec_mix = forward(stack_mixed)
    spec_fil = forward(stack_filter)
    spec_pul = forward(stack_pulled)
    mix_real, mix_imag = (spec_mix[:, 0], spec_mix[:, 1])
    fil_real, fil_imag = (spec_fil[:, 0], spec_fil[:, 1])
    pul_real, pul_imag = (spec_pul[:, 0], spec_pul[:, 1])
    folded_conv = inverse(
        fil_real * mix_real - fil_imag * mix_imag, fil_real * mix_imag + fil_imag * mix_real
    )
    folded_adj = inverse(
        fil_real * pul_real + fil_imag * pul_imag, fil_real * pul_imag - fil_imag * pul_real
    )
    folded_cor = inverse(
        mix_real * pul_real + mix_imag * pul_imag, mix_real * pul_imag - mix_imag * pul_real
    )
    return (folded_conv, folded_adj, folded_cor)


def shards(gate_q, gate_k, value_in, filter_raw, decay_rate, skip_gain, grad_out):
    parts_count = lax.axis_size("ctx")
    my_rank = lax.axis_index("ctx")
    tok_rows = gate_q.shape[1]
    channels = gate_q.shape[2]
    group_rows = tok_rows // parts_count
    seq_length = tok_rows * parts_count
    fft_length = 2 * seq_length
    positions = (my_rank * tok_rows + jnp.arange(tok_rows, dtype=jnp.int32)).astype(
        jnp.float32
    ) / seq_length
    rate_row = decay_rate[0][None, :]
    skip_row = skip_gain[0][None, :]
    envelope = jnp.exp(-rate_row * positions[:, None])
    modulated = filter_raw[0].astype(jnp.float32) * envelope
    filter_bf = modulated.astype(jnp.bfloat16)
    mixed_in = (gate_k[0].astype(jnp.float32) * value_in[0].astype(jnp.float32)).astype(
        jnp.bfloat16
    )
    pulled = (gate_q[0].astype(jnp.float32) * grad_out[0].astype(jnp.float32)).astype(jnp.bfloat16)
    block_shape = (parts_count, group_rows, channels)
    sectioned_mixed, sectioned_filter, sectioned_pulled = (
        lax.all_to_all(
            mixed_in.reshape(block_shape), "ctx", split_axis=0, concat_axis=0, tiled=True
        ),
        lax.all_to_all(
            filter_bf.reshape(block_shape), "ctx", split_axis=0, concat_axis=0, tiled=True
        ),
        lax.all_to_all(pulled.reshape(block_shape), "ctx", split_axis=0, concat_axis=0, tiled=True),
    )
    table_first = every_table(parts_count)

    def first_section(sectioned):
        return jnp.einsum(
            "mgc,mlir->lirgc", sectioned.astype(jnp.float32), table_first, precision=exact_mode
        ).astype(jnp.bfloat16)

    got_mixed, got_filter, got_pulled = (
        lax.all_to_all(
            first_section(sectioned_mixed), "ctx", split_axis=2, concat_axis=2, tiled=True
        ),
        lax.all_to_all(
            first_section(sectioned_filter), "ctx", split_axis=2, concat_axis=2, tiled=True
        ),
        lax.all_to_all(
            first_section(sectioned_pulled), "ctx", split_axis=2, concat_axis=2, tiled=True
        ),
    )

    def unpack(received):
        return received.reshape(2, 2, tok_rows, channels)

    slot_bins = 2 * my_rank + jnp.arange(2, dtype=jnp.int32)
    folded_conv, folded_adj, folded_cor = spectral_middle(
        unpack(got_mixed), unpack(got_filter), unpack(got_pulled), slot_bins, tok_rows, fft_length
    )

    def pack(folded):
        return folded.reshape(2, 2, parts_count, group_rows, channels)

    back_conv, back_adj, back_cor = (
        lax.all_to_all(pack(folded_conv), "ctx", split_axis=2, concat_axis=2, tiled=True),
        lax.all_to_all(pack(folded_adj), "ctx", split_axis=2, concat_axis=2, tiled=True),
        lax.all_to_all(pack(folded_cor), "ctx", split_axis=2, concat_axis=2, tiled=True),
    )
    table_last = table_first / fft_length

    def last_section(received):
        return jnp.einsum(
            "lirgc,mlir->mgc", received.astype(jnp.float32), table_last, precision=exact_mode
        ).astype(jnp.bfloat16)

    home_conv, home_adj, home_cor = (
        lax.all_to_all(last_section(back_conv), "ctx", split_axis=0, concat_axis=0, tiled=True),
        lax.all_to_all(last_section(back_adj), "ctx", split_axis=0, concat_axis=0, tiled=True),
        lax.all_to_all(last_section(back_cor), "ctx", split_axis=0, concat_axis=0, tiled=True),
    )
    conv_out = home_conv.reshape(tok_rows, channels).astype(jnp.float32)
    adjoint = home_adj.reshape(tok_rows, channels).astype(jnp.float32)
    filter_corr = home_cor.reshape(tok_rows, channels).astype(jnp.float32)
    mixed_f = mixed_in.astype(jnp.float32)
    pulled_f = pulled.astype(jnp.float32)
    grad_q_local = (grad_out[0].astype(jnp.float32) * (conv_out + skip_row * mixed_f)).astype(
        jnp.bfloat16
    )
    mixed_grad = adjoint + skip_row * pulled_f
    grad_k_local = (mixed_grad * value_in[0].astype(jnp.float32)).astype(jnp.bfloat16)
    passing = (mixed_grad * gate_k[0].astype(jnp.float32)).astype(jnp.bfloat16)
    passed = shifted(passing[None], "section", -1)
    filter_local = (filter_corr * envelope).astype(jnp.bfloat16)
    rate_part = -jnp.sum(positions[:, None] * filter_corr * modulated, axis=0)
    skip_part = jnp.sum(mixed_f * pulled_f, axis=0)
    rate_total, skip_total = (
        lax.psum(rate_part.astype(jnp.bfloat16), "ctx").astype(jnp.float32),
        lax.psum(skip_part.astype(jnp.bfloat16), "ctx").astype(jnp.float32),
    )
    return (
        grad_q_local[None],
        grad_k_local[None],
        passed,
        filter_local[None],
        rate_total[None],
        skip_total[None],
    )


def solution(mesh):
    in_specs = (
        P("section", "ctx", None),
        P("section", "ctx", None),
        P("section", "ctx", None),
        P("section", "ctx", None),
        P("section", None),
        P("section", None),
        P("section", "ctx", None),
    )
    out_specs = (
        P("section", "ctx", None),
        P("section", "ctx", None),
        P("section", "ctx", None),
        P("section", "ctx", None),
        P("section", None),
        P("section", None),
    )
    return jax.shard_map(shards, mesh=mesh, in_specs=in_specs, out_specs=out_specs, check_vma=False)
```

profile of v0, /device:TPU:0, one launch (start us, length us, event | category | flops | bytes accessed | tf_op | source)
XLA Modules:
  0.0 480.3 jit_solution(238260348380390639)
XLA Ops:
  0.7 0.9 neg.39
  1.6 2.6 fusion.21
  4.2 5.2 %all-to-all-start = ((bf16[4,32,4096]{2,1,0:T(8,128)(2,1)}), bf16[4,32,4096]{2,1,0:T(8,128)(2,1)S(1)}, u32[]{:S(2)}, u32[]{:S(2)}) async-start(bf16[4,32,4096]{2,1,0:T(8,128)(2,1)} %fusion.21), calls=%async_computation | async-start | bytes 2097152 | tf_op jit(solution)/shard_map/all_to_all | solution.py:100
  9.4 3.6 fusion.19
  13.0 10.0 %all-to-all-done = bf16[4,32,4096]{2,1,0:T(8,128)(2,1)S(1)} async-done(((bf16[4,32,4096]{2,1,0:T(8,128)(2,1)}), bf16[4,32,4096]{2,1,0:T(8,128)(2,1)S(1)}, u32[]{:S(2)}, u32[]{:S(2)}) %all-to-all-start) | async-done | bytes 1048608 | tf_op jit(solution)/shard_map/all_to_all | solution.py:100
  23.0 3.5 all-to-all-start.6
  26.5 13.1 %all-to-all-done.6 = bf16[4,32,4096]{2,1,0:T(8,128)(2,1)S(1)} async-done(((bf16[4,32,4096]{2,1,0:T(8,128)(2,1)}), bf16[4,32,4096]{2,1,0:T(8,128)(2,1)S(1)}, u32[]{:S(2)}, u32[]{:S(2)}) %all-to-all-start.6) | async-done | bytes 1048608 | tf_op jit(solution)/shard_map/all_to_all | solution.py:103
  39.6 3.5 all-to-all-start.2
  43.2 6.4 %convolution_convert_fusion = bf16[2,2,4,32,4096]{4,2,3,1,0:T(4,128)(2,1)S(1)} fusion(bf16[4,32,4096,1,1]{2,1,0,4,3:T(8,128)(2,1)S(1)} %bitcast.132, f32[4,2,1,4]{0,3,2,1:T(4,128)S(1)} %get-tuple-element.33, f32[4,2,1,4]{0,3,2,1:T(4,128)S(1)} %get-tuple-element.32), kind=kOutput, calls=%fused_computation.15 | convolution fusion | flops 102760512 | bytes 5243136 | tf_op jit(solution)/shard_map/mgc,mlir->lirgc/dot_general | solution.py:108
  49.6 4.3 copy.56
  53.9 2.2 all-to-all-done.2
  56.2 5.0 %all-to-all-start.7 = ((bf16[2,2,4,32,4096]{4,3,1,0,2:T(8,128)(2,1)}), bf16[2,2,4,32,4096]{4,3,1,0,2:T(8,128)(2,1)}, u32[]{:S(2)}, u32[]{:S(2)}) async-start(bf16[2,2,4,32,4096]{4,3,1,0,2:T(8,128)(2,1)} %copy.56), calls=%async_computation.7 | async-start | bytes 8388608 | tf_op jit(solution)/shard_map/all_to_all | solution.py:119
  61.2 6.4 %convolution_convert_fusion.2 = bf16[2,2,4,32,4096]{4,2,3,1,0:T(4,128)(2,1)S(1)} fusion(bf16[4,32,4096,1,1]{2,1,0,4,3:T(8,128)(2,1)S(1)} %bitcast.128, f32[4,2,1,4]{0,3,2,1:T(4,128)S(1)} %get-tuple-element.33, f32[4,2,1,4]{0,3,2,1:T(4,128)S(1)} %get-tuple-element.32), kind=kOutput, calls=%fused_computation.17 | convolution fusion | flops 102760512 | bytes 5243136 | tf_op jit(solution)/shard_map/mgc,mlir->lirgc/dot_general | solution.py:108
  67.6 4.3 copy.44
  71.9 36.1 %all-to-all-done.7 = bf16[2,2,4,32,4096]{4,3,1,0,2:T(8,128)(2,1)} async-done(((bf16[2,2,4,32,4096]{4,3,1,0,2:T(8,128)(2,1)}), bf16[2,2,4,32,4096]{4,3,1,0,2:T(8,128)(2,1)}, u32[]{:S(2)}, u32[]{:S(2)}) %all-to-all-start.7) | async-done | bytes 4194336 | tf_op jit(solution)/shard_map/all_to_all | solution.py:119
  108.0 5.1 %all-to-all-start.1 = ((bf16[2,2,4,32,4096]{4,3,1,0,2:T(8,128)(2,1)}), bf16[2,2,4,32,4096]{4,3,1,0,2:T(8,128)(2,1)}, u32[]{:S(2)}, u32[]{:S(2)}) async-start(bf16[2,2,4,32,4096]{4,3,1,0,2:T(8,128)(2,1)} %copy.44), calls=%async_computation.1 | async-start | bytes 8388608 | tf_op jit(solution)/shard_map/all_to_all | solution.py:116
  113.1 6.4 %convolution_convert_fusion.1 = bf16[2,2,4,32,4096]{4,2,3,1,0:T(4,128)(2,1)S(1)} fusion(bf16[4,32,4096,1,1]{2,1,0,4,3:T(8,128)(2,1)S(1)} %bitcast.130, f32[4,2,1,4]{0,3,2,1:T(4,128)S(1)} %get-tuple-element.33, f32[4,2,1,4]{0,3,2,1:T(4,128)S(1)} %get-tuple-element.32), kind=kOutput, calls=%fused_computation.16 | convolution fusion | flops 102760512 | bytes 5243136 | tf_op jit(solution)/shard_map/mgc,mlir->lirgc/dot_general | solution.py:108
  119.5 4.3 copy.47
  123.8 36.2 %all-to-all-done.1 = bf16[2,2,4,32,4096]{4,3,1,0,2:T(8,128)(2,1)} async-done(((bf16[2,2,4,32,4096]{4,3,1,0,2:T(8,128)(2,1)}), bf16[2,2,4,32,4096]{4,3,1,0,2:T(8,128)(2,1)}, u32[]{:S(2)}, u32[]{:S(2)}) %all-to-all-start.1) | async-done | bytes 4194336 | tf_op jit(solution)/shard_map/all_to_all | solution.py:116
  160.0 5.3 %all-to-all-start.3 = ((bf16[2,2,4,32,4096]{4,3,1,0,2:T(8,128)(2,1)}), bf16[2,2,4,32,4096]{4,3,1,0,2:T(8,128)(2,1)}, u32[]{:S(2)}, u32[]{:S(2)}) async-start(bf16[2,2,4,32,4096]{4,3,1,0,2:T(8,128)(2,1)} %copy.47), calls=%async_computation.3 | async-start | bytes 8388608 | tf_op jit(solution)/shard_map/all_to_all | solution.py:113
  165.4 1.1 fusion.39
  166.6 2.5 copy.57
  169.1 2.5 copy.45
  171.5 5.6 %convolution_bitcast_fusion.2 = f32[2,2,128,4096]{3,2,1,0:T(8,128)} fusion(bf16[2,2,128,4096,1]{3,2,1,4,0:T(8,128)(2,1)S(1)} %bitcast.121, f32[2,1,128,2,128]{2,4,1,3,0:T(8,128)S(1)} %get-tuple-element.24, f32[2,1,128,2,128]{2,4,1,3,0:T(8,128)S(1)} %get-tuple-element.23), kind=kOutput, calls=%fused_computation.14 | convolution fusion | flops 6442582016 | bytes 13107200 | tf_op jit(solution)/shard_map/spjc,spjqb->sqbc/dot_general | solution.py:47
  177.1 5.7 %convolution_bitcast_fusion = f32[2,2,128,4096]{3,2,1,0:T(8,128)} fusion(bf16[2,2,128,4096,1]{3,2,1,4,0:T(8,128)(2,1)S(1)} %bitcast.119, f32[2,1,128,2,128]{2,4,1,3,0:T(8,128)S(1)} %get-tuple-element.24, f32[2,1,128,2,128]{2,4,1,3,0:T(8,128)S(1)} %get-tuple-element.23), kind=kOutput, calls=%fused_computation.12 | convolution fusion | flops 6442582016 | bytes 13107200 | tf_op jit(solution)/shard_map/spjc,spjqb->sqbc/dot_general | solution.py:47
  182.8 29.4 %all-to-all-done.3 = bf16[2,2,4,32,4096]{4,3,1,0,2:T(8,128)(2,1)} async-done(((bf16[2,2,4,32,4096]{4,3,1,0,2:T(8,128)(2,1)}), bf16[2,2,4,32,4096]{4,3,1,0,2:T(8,128)(2,1)}, u32[]{:S(2)}, u32[]{:S(2)}) %all-to-all-start.3) | async-done | bytes 4194336 | tf_op jit(solution)/shard_map/all_to_all | solution.py:113
  212.2 2.6 copy.48
  214.8 5.7 %convolution_bitcast_fusion.1 = f32[2,2,128,4096]{3,2,1,0:T(8,128)} fusion(bf16[2,2,128,4096,1]{3,2,1,4,0:T(8,128)(2,1)S(1)} %bitcast.120, f32[2,1,128,2,128]{2,4,1,3,0:T(8,128)S(1)} %get-tuple-element.24, f32[2,1,128,2,128]{2,4,1,3,0:T(8,128)S(1)} %get-tuple-element.23), kind=kOutput, calls=%fused_computation.13 | convolution fusion | flops 6442582016 | bytes 13107200 | tf_op jit(solution)/shard_map/spjc,spjqb->sqbc/dot_general | solution.py:47
  220.5 11.1 %multiply_add_fusion = (f32[2,1,128,4096]{3,2,1,0:T(8,128)S(1)}, f32[2,1,128,4096]{3,2,1,0:T(8,128)}, f32[2,1,128,4096]{3,2,1,0:T(8,128)}, f32[2,1,128,4096]{3,2,1,0:T(8,128)}) fusion(f32[2,2,128,4096]{3,2,1,0:T(8,128)} %convolution_bitcast_fusion, f32[2,2,128,4096]{3,2,1,0:T(8,128)} %convolution_bitcast_fusion.1, f32[2,2,128,4096]{3,2,1,0:T(8,128)S(1)} %bitcast.118), kind=kLoop, calls=%fused_computation.25 | loop fusion | flops 12582912 | bytes 41943040 | tf_op jit(solution)/shard_map/add | solution.py:70
  231.7 7.5 %maximum_bitcast_fusion = (f32[2,2,128,4096,1]{3,2,1,0,4:T(8,128)S(1)}, f32[2,2,128,4096,1]{3,2,1,0,4:T(8,128)}) fusion(f32[2,1,128,4096]{3,2,1,0:T(8,128)} %get-tuple-element.17, f32[2,1,128,4096]{3,2,1,0:T(8,128)} %get-tuple-element.18, f32[2,1,128,4096]{3,2,1,0:T(8,128)} %get-tuple-element.12, f32[2,1,128,4096]{3,2,1,0:T(8,128)S(1)} %get-tuple-element.11), kind=kLoop, calls=%fused_computation | loop fusion | flops 4194304 | bytes 33554432 | tf_op jit(solution)/shard_map/stack | solution.py:52
  239.2 8.0 %fusion.4 = bf16[2,2,128,4096,1]{3,2,1,0,4:T(8,128)(2,1)S(1)} fusion(f32[2,2,128,4096,1]{3,2,1,0,4:T(8,128)S(1)} %get-tuple-element.34, f32[2,1,128,2,128]{2,4,3,0,1:T(8,128)S(1)} %get-tuple-element.22, f32[2,1,128,2,128]{2,4,3,0,1:T(8,128)S(1)} %get-tuple-element.21), kind=kOutput, calls=%fused_computation.10 | convolution fusion | flops 6442582016 | bytes 13107200 | tf_op jit(solution)/shard_map/sqbc,sqbpj->spjc/dot_general | solution.py:53
  247.2 0.5 copy.136
  247.6 6.3 %copy.51 = bf16[2,2,4,32,4096]{4,0,1,3,2:T(2,128)(2,1)} copy(bf16[2,2,4,32,4096]{4,3,2,0,1:T(8,128)(2,1)S(1)} %bitcast.122) | data formatting | bytes 8388608 | tf_op jit(solution)/shard_map/reshape | solution.py:133
  254.0 5.1 %all-to-all-start.4 = ((bf16[2,2,4,32,4096]{4,0,1,3,2:T(2,128)(2,1)}), bf16[2,2,4,32,4096]{4,0,1,3,2:T(2,128)(2,1)}, u32[]{:S(2)}, u32[]{:S(2)}) async-start(bf16[2,2,4,32,4096]{4,0,1,3,2:T(2,128)(2,1)} %copy.51), calls=%async_computation.4 | async-start | bytes 8388608 | tf_op jit(solution)/shard_map/all_to_all | solution.py:136
  259.1 9.2 %fusion = bf16[2,2,128,4096,1]{3,2,1,0,4:T(8,128)(2,1)S(1)} fusion(f32[2,2,128,4096,1]{3,2,1,0,4:T(8,128)} %get-tuple-element.35, f32[2,1,128,2,128]{2,4,3,0,1:T(8,128)S(1)} %get-tuple-element.22, f32[2,1,128,2,128]{2,4,3,0,1:T(8,128)S(1)} %get-tuple-element.21), kind=kOutput, calls=%fused_computation.4 | convolution fusion | flops 6442582016 | bytes 13107200 | tf_op jit(solution)/shard_map/sqbc,sqbpj->spjc/dot_general | solution.py:53
  268.8 6.4 %copy.66 = bf16[2,2,4,32,4096]{4,0,1,3,2:T(2,128)(2,1)} copy(bf16[2,2,4,32,4096]{4,3,2,0,1:T(8,128)(2,1)S(1)} %bitcast.123) | data formatting | bytes 8388608 | tf_op jit(solution)/shard_map/reshape | solution.py:133
  275.2 30.8 %all-to-all-done.4 = bf16[2,2,4,32,4096]{4,0,1,3,2:T(2,128)(2,1)} async-done(((bf16[2,2,4,32,4096]{4,0,1,3,2:T(2,128)(2,1)}), bf16[2,2,4,32,4096]{4,0,1,3,2:T(2,128)(2,1)}, u32[]{:S(2)}, u32[]{:S(2)}) %all-to-all-start.4) | async-done | bytes 4194336 | tf_op jit(solution)/shard_map/all_to_all | solution.py:136
  306.0 5.1 %all-to-all-start.10 = ((bf16[2,2,4,32,4096]{4,0,1,3,2:T(2,128)(2,1)}), bf16[2,2,4,32,4096]{4,0,1,3,2:T(2,128)(2,1)}, u32[]{:S(2)}, u32[]{:S(2)}) async-start(bf16[2,2,4,32,4096]{4,0,1,3,2:T(2,128)(2,1)} %copy.66), calls=%async_computation.10 | async-start | bytes 8388608 | tf_op jit(solution)/shard_map/all_to_all | solution.py:138
  311.1 6.5 %multiply_add_fusion.1 = (f32[2,1,128,4096]{3,2,1,0:T(8,128)S(1)}, f32[2,1,128,4096]{3,2,1,0:T(8,128)S(1)}) fusion(f32[2,2,128,4096]{3,2,1,0:T(8,128)} %convolution_bitcast_fusion, f32[2,2,128,4096]{3,2,1,0:T(8,128)} %convolution_bitcast_fusion.2), kind=kLoop, calls=%fused_computation.27 | loop fusion | flops 6291456 | bytes 25165824 | tf_op jit(solution)/shard_map/add | solution.py:67
  317.7 7.8 %fusion.2 = bf16[2,2,128,4096,1]{3,2,1,0,4:T(8,128)(2,1)S(1)} fusion(f32[2,1,128,2,128]{2,4,3,0,1:T(8,128)S(1)} %get-tuple-element.22, f32[2,1,128,2,128]{2,4,3,0,1:T(8,128)S(1)} %get-tuple-element.21, f32[2,1,128,4096]{3,2,1,0:T(8,128)S(1)} %get-tuple-element.14, f32[2,1,128,4096]{3,2,1,0:T(8,128)S(1)} %get-tuple-element.13), kind=kOutput, calls=%fused_computation.7 | convolution fusion | flops 6444679168 | bytes 13107200 | tf_op jit(solution)/shard_map/sqbc,sqbpj->spjc/dot_general | solution.py:53
  326.0 6.3 %copy.60 = bf16[2,2,4,32,4096]{4,0,1,3,2:T(2,128)(2,1)} copy(bf16[2,2,4,32,4096]{4,3,2,0,1:T(8,128)(2,1)S(1)} %bitcast.124) | data formatting | bytes 8388608 | tf_op jit(solution)/shard_map/reshape | solution.py:133
  332.3 25.7 %all-to-all-done.10 = bf16[2,2,4,32,4096]{4,0,1,3,2:T(2,128)(2,1)} async-done(((bf16[2,2,4,32,4096]{4,0,1,3,2:T(2,128)(2,1)}), bf16[2,2,4,32,4096]{4,0,1,3,2:T(2,128)(2,1)}, u32[]{:S(2)}, u32[]{:S(2)}) %all-to-all-start.10) | async-done | bytes 4194336 | tf_op jit(solution)/shard_map/all_to_all | solution.py:138
  358.0 5.4 %all-to-all-start.8 = ((bf16[2,2,4,32,4096]{4,0,1,3,2:T(2,128)(2,1)}), bf16[2,2,4,32,4096]{4,0,1,3,2:T(2,128)(2,1)}, u32[]{:S(2)}, u32[]{:S(2)}) async-start(bf16[2,2,4,32,4096]{4,0,1,3,2:T(2,128)(2,1)} %copy.60), calls=%async_computation.8 | async-start | bytes 8388608 | tf_op jit(solution)/shard_map/all_to_all | solution.py:137
  363.4 10.8 %fusion.6 = bf16[4,32,4096]{2,0,1:T(4,128)(2,1)S(1)} fusion(bf16[2,2,4,32,4096]{4,0,1,3,2:T(2,128)(2,1)} %all-to-all-done.4, f32[4,2,1,4]{0,3,2,1:T(4,128)S(1)} %get-tuple-element.33, f32[4,2,1,4]{0,3,2,1:T(4,128)S(1)} %get-tuple-element.32), kind=kOutput, calls=%fused_computation.21 | convolution fusion | flops 101187712 | bytes 5243136 | tf_op jit(solution)/shard_map/lirgc,mlir->mgc/dot_general | solution.py:143
  374.2 1.6 copy.54
  375.7 34.5 %all-to-all-done.8 = bf16[2,2,4,32,4096]{4,0,1,3,2:T(2,128)(2,1)} async-done(((bf16[2,2,4,32,4096]{4,0,1,3,2:T(2,128)(2,1)}), bf16[2,2,4,32,4096]{4,0,1,3,2:T(2,128)(2,1)}, u32[]{:S(2)}, u32[]{:S(2)}) %all-to-all-start.8) | async-done | bytes 4194336 | tf_op jit(solution)/shard_map/all_to_all | solution.py:137
  410.2 3.5 all-to-all-start.5
  413.8 10.8 %fusion.7 = bf16[4,32,4096]{2,0,1:T(4,128)(2,1)S(1)} fusion(bf16[2,2,4,32,4096]{4,0,1,3,2:T(2,128)(2,1)} %all-to-all-done.8, f32[4,2,1,4]{0,3,2,1:T(4,128)S(1)} %get-tuple-element.33, f32[4,2,1,4]{0,3,2,1:T(4,128)S(1)} %get-tuple-element.32), kind=kOutput, calls=%fused_computation.22 | convolution fusion | flops 101187712 | bytes 5243136 | tf_op jit(solution)/shard_map/lirgc,mlir->mgc/dot_general | solution.py:143
  424.6 1.6 copy.63
  426.1 0.7 all-to-all-done.5
  426.9 3.7 all-to-all-start.9
  430.6 10.8 %fusion.8 = bf16[4,32,4096]{2,0,1:T(4,128)(2,1)S(1)} fusion(bf16[2,2,4,32,4096]{4,0,1,3,2:T(2,128)(2,1)} %all-to-all-done.10, f32[4,2,1,4]{0,3,2,1:T(4,128)S(1)} %get-tuple-element.33, f32[4,2,1,4]{0,3,2,1:T(4,128)S(1)} %get-tuple-element.32), kind=kOutput, calls=%fused_computation.23 | convolution fusion | flops 101187712 | bytes 5243136 | tf_op jit(solution)/shard_map/lirgc,mlir->mgc/dot_general | solution.py:143
  441.4 1.6 copy.69
  443.0 0.6 all-to-all-done.9
  443.6 3.6 all-to-all-start.11
  447.2 5.5 %fusion.14 = (bf16[1,128,4096]{2,1,0:T(8,128)(2,1)}, bf16[1,128,4096]{2,1,0:T(8,128)(2,1)}, bf16[1,128,4096]{2,1,0:T(8,128)(2,1)}) fusion(bf16[1,128,4096]{2,1,0:T(8,128)(2,1)} %param.8, bf16[1,128,4096]{2,1,0:T(8,128)(2,1)} %get-tuple-element.9, f32[4096]{0:T(1024)S(1)} %bitcast.136, bf16[1,128,4096]{2,1,0:T(8,128)(2,1)} %param.9, ...), kind=kLoop, calls=%fused_computation.43 | loop fusion | flops 8912896 | bytes 10502144 | tf_op jit(solution)/shard_map/convert_element_type | solution.py:162
  452.7 1.3 collective-permute-start
  454.0 6.2 %all-to-all-done.11 = bf16[4,32,4096]{2,1,0:T(8,128)(2,1)S(1)} async-done(((bf16[4,32,4096]{2,1,0:T(8,128)(2,1)}), bf16[4,32,4096]{2,1,0:T(8,128)(2,1)S(1)}, u32[]{:S(2)}, u32[]{:S(2)}) %all-to-all-start.11) | async-done | bytes 1048608 | tf_op jit(solution)/shard_map/all_to_all | solution.py:150
  460.2 0.7 multiply_reduce_fusion
  461.0 15.3 %all-reduce = (bf16[1,4096]{1,0:T(2,128)(2,1)S(1)}, bf16[1,4096]{1,0:T(2,128)(2,1)S(1)}) all-reduce(bf16[1,4096]{1,0:T(2,128)(2,1)S(1)} %broadcast_in_dim.10, bf16[1,4096]{1,0:T(2,128)(2,1)S(1)} %broadcast_in_dim.12), channel_id=1, replica_groups=mesh['section'=8,'ctx'=4] {'ctx'}, use_global_device_ids=true, to_apply=%region_1.2 | all-reduce | flops 8192 | bytes 32768 | tf_op jit(solution)/shard_map/psum | solution.py:168
  476.3 0.6 broadcast_in_dim.11
  476.9 0.6 broadcast_in_dim.13
  477.8 1.4 fusion.20
  479.1 1.0 copy.138
  (31 shorter events, 1.5 us)
Async XLA Ops:
  0.6 8.7 %copy-start.3 = (bf16[1,128,4096]{2,1,0:T(8,128)(2,1)S(1)}, bf16[1,128,4096]{2,1,0:T(8,128)(2,1)}, u32[]{:S(2)}) copy-start(bf16[1,128,4096]{2,1,0:T(8,128)(2,1)} %param.13) | copy-start | bytes 3145732
  0.6 8.7 %copy-start.2 = (bf16[1,128,4096]{2,1,0:T(8,128)(2,1)S(1)}, bf16[1,128,4096]{2,1,0:T(8,128)(2,1)}, u32[]{:S(2)}) copy-start(bf16[1,128,4096]{2,1,0:T(8,128)(2,1)} %param.8) | copy-start | bytes 3145732
  4.2 18.8 %all-to-all-start = ((bf16[4,32,4096]{2,1,0:T(8,128)(2,1)}), bf16[4,32,4096]{2,1,0:T(8,128)(2,1)S(1)}, u32[]{:S(2)}, u32[]{:S(2)}) async-start(bf16[4,32,4096]{2,1,0:T(8,128)(2,1)} %fusion.21), calls=%async_computation | async-start | bytes 2097152 | tf_op jit(solution)/shard_map/all_to_all | solution.py:100
  23.0 16.6 %all-to-all-start.6 = ((bf16[4,32,4096]{2,1,0:T(8,128)(2,1)}), bf16[4,32,4096]{2,1,0:T(8,128)(2,1)S(1)}, u32[]{:S(2)}, u32[]{:S(2)}) async-start(bf16[4,32,4096]{2,1,0:T(8,128)(2,1)} %bitcast.32), calls=%async_computation.6 | async-start | bytes 2097152 | tf_op jit(solution)/shard_map/all_to_all | solution.py:103
  39.6 16.6 %all-to-all-start.2 = ((bf16[4,32,4096]{2,1,0:T(8,128)(2,1)}), bf16[4,32,4096]{2,1,0:T(8,128)(2,1)S(1)}, u32[]{:S(2)}, u32[]{:S(2)}) async-start(bf16[4,32,4096]{2,1,0:T(8,128)(2,1)} %bitcast.17), calls=%async_computation.2 | async-start | bytes 2097152 | tf_op jit(solution)/shard_map/all_to_all | solution.py:97
  56.2 51.9 %all-to-all-start.7 = ((bf16[2,2,4,32,4096]{4,3,1,0,2:T(8,128)(2,1)}), bf16[2,2,4,32,4096]{4,3,1,0,2:T(8,128)(2,1)}, u32[]{:S(2)}, u32[]{:S(2)}) async-start(bf16[2,2,4,32,4096]{4,3,1,0,2:T(8,128)(2,1)} %copy.56), calls=%async_computation.7 | async-start | bytes 8388608 | tf_op jit(solution)/shard_map/all_to_all | solution.py:119
  108.0 52.0 %all-to-all-start.1 = ((bf16[2,2,4,32,4096]{4,3,1,0,2:T(8,128)(2,1)}), bf16[2,2,4,32,4096]{4,3,1,0,2:T(8,128)(2,1)}, u32[]{:S(2)}, u32[]{:S(2)}) async-start(bf16[2,2,4,32,4096]{4,3,1,0,2:T(8,128)(2,1)} %copy.44), calls=%async_computation.1 | async-start | bytes 8388608 | tf_op jit(solution)/shard_map/all_to_all | solution.py:116
  160.0 52.2 %all-to-all-start.3 = ((bf16[2,2,4,32,4096]{4,3,1,0,2:T(8,128)(2,1)}), bf16[2,2,4,32,4096]{4,3,1,0,2:T(8,128)(2,1)}, u32[]{:S(2)}, u32[]{:S(2)}) async-start(bf16[2,2,4,32,4096]{4,3,1,0,2:T(8,128)(2,1)} %copy.47), calls=%async_computation.3 | async-start | bytes 8388608 | tf_op jit(solution)/shard_map/all_to_all | solution.py:113
  212.2 8.3 %slice-start = ((s8[8388608]{0:T(1024)(128)(4,1)}), s8[4194304]{0:T(1024)(128)(4,1)S(1)}, s32[]{:S(2)}) async-start(s8[8388608]{0:T(1024)(128)(4,1)} %bitcast.117), calls=%async_computation.12 | async-start | bytes 8388608
  214.8 5.7 %slice-start.1 = ((s8[8388608]{0:T(1024)(128)(4,1)}), s8[4194304]{0:T(1024)(128)(4,1)S(1)}, s32[]{:S(2)}) async-start(s8[8388608]{0:T(1024)(128)(4,1)} %bitcast.117), calls=%async_computation.13 | async-start | bytes 8388608
  254.0 52.0 %all-to-all-start.4 = ((bf16[2,2,4,32,4096]{4,0,1,3,2:T(2,128)(2,1)}), bf16[2,2,4,32,4096]{4,0,1,3,2:T(2,128)(2,1)}, u32[]{:S(2)}, u32[]{:S(2)}) async-start(bf16[2,2,4,32,4096]{4,0,1,3,2:T(2,128)(2,1)} %copy.51), calls=%async_computation.4 | async-start | bytes 8388608 | tf_op jit(solution)/shard_map/all_to_all | solution.py:136
  306.0 52.0 %all-to-all-start.10 = ((bf16[2,2,4,32,4096]{4,0,1,3,2:T(2,128)(2,1)}), bf16[2,2,4,32,4096]{4,0,1,3,2:T(2,128)(2,1)}, u32[]{:S(2)}, u32[]{:S(2)}) async-start(bf16[2,2,4,32,4096]{4,0,1,3,2:T(2,128)(2,1)} %copy.66), calls=%async_computation.10 | async-start | bytes 8388608 | tf_op jit(solution)/shard_map/all_to_all | solution.py:138
  358.0 52.3 %all-to-all-start.8 = ((bf16[2,2,4,32,4096]{4,0,1,3,2:T(2,128)(2,1)}), bf16[2,2,4,32,4096]{4,0,1,3,2:T(2,128)(2,1)}, u32[]{:S(2)}, u32[]{:S(2)}) async-start(bf16[2,2,4,32,4096]{4,0,1,3,2:T(2,128)(2,1)} %copy.60), calls=%async_computation.8 | async-start | bytes 8388608 | tf_op jit(solution)/shard_map/all_to_all | solution.py:137
  410.2 16.6 %all-to-all-start.5 = ((bf16[4,32,4096]{2,1,0:T(8,128)(2,1)}), bf16[4,32,4096]{2,1,0:T(8,128)(2,1)S(1)}, u32[]{:S(2)}, u32[]{:S(2)}) async-start(bf16[4,32,4096]{2,1,0:T(8,128)(2,1)} %copy.54), calls=%async_computation.5 | async-start | bytes 2097152 | tf_op jit(solution)/shard_map/all_to_all | solution.py:148
  426.9 16.7 %all-to-all-start.9 = ((bf16[4,32,4096]{2,1,0:T(8,128)(2,1)}), bf16[4,32,4096]{2,1,0:T(8,128)(2,1)S(1)}, u32[]{:S(2)}, u32[]{:S(2)}) async-start(bf16[4,32,4096]{2,1,0:T(8,128)(2,1)} %copy.63), calls=%async_computation.9 | async-start | bytes 2097152 | tf_op jit(solution)/shard_map/all_to_all | solution.py:149
  441.4 5.7 %copy-start.4 = (f32[1,4096]{1,0:T(1,128)S(1)}, f32[1,4096]{1,0:T(1,128)}, u32[]{:S(2)}) copy-start(f32[1,4096]{1,0:T(1,128)} %param.12) | copy-start | bytes 49156
  443.6 3.6 copy-start.1
  443.6 16.6 %all-to-all-start.11 = ((bf16[4,32,4096]{2,1,0:T(8,128)(2,1)}), bf16[4,32,4096]{2,1,0:T(8,128)(2,1)S(1)}, u32[]{:S(2)}, u32[]{:S(2)}) async-start(bf16[4,32,4096]{2,1,0:T(8,128)(2,1)} %copy.69), calls=%async_computation.11 | async-start | bytes 2097152 | tf_op jit(solution)/shard_map/all_to_all | solution.py:150
  447.2 13.0 %copy-start = (bf16[1,128,4096]{2,1,0:T(8,128)(2,1)S(1)}, bf16[1,128,4096]{2,1,0:T(8,128)(2,1)}, u32[]{:S(2)}) copy-start(bf16[1,128,4096]{2,1,0:T(8,128)(2,1)} %param.10) | copy-start | bytes 3145732
  452.7 26.4 %collective-permute-start = (bf16[1,128,4096]{2,1,0:T(8,128)(2,1)}, bf16[1,128,4096]{2,1,0:T(8,128)(2,1)S(1)}, u32[]{:S(2)}, u32[]{:S(2)}) collective-permute-start(bf16[1,128,4096]{2,1,0:T(8,128)(2,1)} %get-tuple-element.19), channel_id=1, source_target_pairs={{4,0},{8,4},{12,8},{16,12},{20,16},{24,20},{28,24},{5,1},{9,5},{13... | collective-permute-start | bytes 3145736 | tf_op jit(solution)/shard_map/ppermute | solution.py:13
where the time goes:
time: 489 us; the launch traced here: 480 us
  waiting for transfers between devices  226 us (46%)
  matrix products  93.4 us (19%)
  starting transfers between devices  55.3 us (11%)
  local copies, waits for them, and re-layouts  46.6 us (10%)
  other arithmetic  42.8 us (9%)
  blocking collectives  15.3 us (3%)
    all_to_all x1, waiting for transfers between devices, shards(): lax.all_to_all(first_section(sectioned_filter), 'ctx', split_axis=2, conc...  36.2 us
    all_to_all x1, waiting for transfers between devices, shards(): lax.all_to_all(first_section(sectioned_pulled), 'ctx', split_axis=2, conc...  36.1 us
    all_to_all x1, waiting for transfers between devices, shards(): lax.all_to_all(pack(folded_adj), 'ctx', split_axis=2, concat_axis=2, tile...  34.5 us
    dot_general x3, matrix products, last_section(): jnp.einsum('lirgc,mlir->mgc', received.astype(jnp.float32), table_last, p...  32.4 us
    all_to_all x1, waiting for transfers between devices, shards(): lax.all_to_all(pack(folded_conv), 'ctx', split_axis=2, concat_axis=2, til...  30.8 us
    all_to_all x1, waiting for transfers between devices, shards(): lax.all_to_all(first_section(sectioned_mixed), 'ctx', split_axis=2, conca...  29.4 us
    all_to_all x1, waiting for transfers between devices, shards(): lax.all_to_all(pack(folded_cor), 'ctx', split_axis=2, concat_axis=2, tile...  25.7 us
    dot_general x3, matrix products, inverse(): jnp.einsum('sqbc,sqbpj->spjc', stacked, inverse_table, precision=exact_mode)  25 us
  transfers between devices with their start and end apart: 13, of which 12 were waited for; matrix products, arithmetic and copies ran while one was open for 28% of the time, Pallas kernels for 0%

commit v1 on v0

--- a/solution.py
+++ b/solution.py
@@ -133,7 +133,15 @@
         return folded.reshape(2, 2, parts_count, group_rows, channels)
 
     back_conv, back_adj, back_cor = (
-        lax.all_to_all(pack(folded_conv), "ctx", split_axis=2, concat_axis=2, tiled=True),
+        jnp.concatenate(
+            lax.all_to_all(
+                jnp.stack(jnp.split(pack(folded_conv), lax.axis_size("ctx"), 2), axis=0),
+                "ctx",
+                0,
+                0,
+            ),
+            2,
+        ),
         lax.all_to_all(pack(folded_adj), "ctx", split_axis=2, concat_axis=2, tiled=True),
         lax.all_to_all(pack(folded_cor), "ctx", split_axis=2, concat_axis=2, tiled=True),
     )

time: 489 us -> 489 us (level)
    another operation x0 -> x1, local copies, waits for them, and re-layouts: none -> 6.38 us  [shards(): jnp.stack(jnp.split(pack(folded_conv), lax.axis_size('ctx'), 2), axis=0)]
    reshape x3 -> x2, local copies, waits for them, and re-layouts: 19.1 us -> 12.8 us  [pack(): return folded.reshape(2, 2, parts_count, group_rows, channels)]
    all_to_all x1, waiting for transfers between devices: 34.5 us -> 29.6 us  [shards(): lax.all_to_all(pack(folded_adj), 'ctx', split_axis=2, concat_axis=2, tile...]
  transfers between devices with their start and end apart: 13 -> 13, of which waited for: 12 -> 12; matrix products, arithmetic and copies ran while one was open for 28% -> 29% of each run, Pallas kernels for 0% -> 0%
where the time goes in v1:
time: 489 us; the launch traced here: 480 us
  waiting for transfers between devices  224 us (46%)
  matrix products  93.5 us (19%)
  starting transfers between devices  55.2 us (11%)
  local copies, waits for them, and re-layouts  47.3 us (10%)
  other arithmetic  43.4 us (9%)
  blocking collectives  15.3 us (3%)
    all_to_all x1, waiting for transfers between devices, shards(): lax.all_to_all(first_section(sectioned_filter), 'ctx', split_axis=2, conc...  36.2 us
    all_to_all x1, waiting for transfers between devices, shards(): lax.all_to_all(first_section(sectioned_pulled), 'ctx', split_axis=2, conc...  36.1 us
    all_to_all x1, waiting for transfers between devices, shards(): lax.all_to_all(jnp.stack(jnp.split(pack(folded_conv), lax.axis_size('ctx'...  34.5 us
    dot_general x3, matrix products, last_section(): jnp.einsum('lirgc,mlir->mgc', received.astype(jnp.float32), table_last, p...  32.4 us
    all_to_all x1, waiting for transfers between devices, shards(): lax.all_to_all(pack(folded_adj), 'ctx', split_axis=2, concat_axis=2, tile...  29.6 us
    all_to_all x1, waiting for transfers between devices, shards(): lax.all_to_all(first_section(sectioned_mixed), 'ctx', split_axis=2, conca...  29.4 us
    all_to_all x1, waiting for transfers between devices, shards(): lax.all_to_all(pack(folded_cor), 'ctx', split_axis=2, concat_axis=2, tile...  25.6 us
    dot_general x3, matrix products, inverse(): jnp.einsum('sqbc,sqbpj->spjc', stacked, inverse_table, precision=exact_mode)  25 us
  transfers between devices with their start and end apart: 13, of which 12 were waited for; matrix products, arithmetic and copies ran while one was open for 29% of the time, Pallas kernels for 0%

profile of v1, /device:TPU:0, one launch (start us, length us, event | category | flops | bytes accessed | tf_op | source)
XLA Modules:
  0.0 480.3 jit_solution(15390053669320951833)
XLA Ops:
  0.7 0.9 neg.39
  1.6 2.6 fusion.22
  4.2 5.2 %all-to-all-start = ((bf16[4,32,4096]{2,1,0:T(8,128)(2,1)}), bf16[4,32,4096]{2,1,0:T(8,128)(2,1)S(1)}, u32[]{:S(2)}, u32[]{:S(2)}) async-start(bf16[4,32,4096]{2,1,0:T(8,128)(2,1)} %fusion.22), calls=%async_computation | async-start | bytes 2097152 | tf_op jit(solution)/shard_map/all_to_all | solution.py:100
  9.4 3.6 fusion.20
  13.0 10.0 %all-to-all-done = bf16[4,32,4096]{2,1,0:T(8,128)(2,1)S(1)} async-done(((bf16[4,32,4096]{2,1,0:T(8,128)(2,1)}), bf16[4,32,4096]{2,1,0:T(8,128)(2,1)S(1)}, u32[]{:S(2)}, u32[]{:S(2)}) %all-to-all-start) | async-done | bytes 1048608 | tf_op jit(solution)/shard_map/all_to_all | solution.py:100
  23.0 3.5 all-to-all-start.6
  26.5 13.1 %all-to-all-done.6 = bf16[4,32,4096]{2,1,0:T(8,128)(2,1)S(1)} async-done(((bf16[4,32,4096]{2,1,0:T(8,128)(2,1)}), bf16[4,32,4096]{2,1,0:T(8,128)(2,1)S(1)}, u32[]{:S(2)}, u32[]{:S(2)}) %all-to-all-start.6) | async-done | bytes 1048608 | tf_op jit(solution)/shard_map/all_to_all | solution.py:103
  39.6 3.5 all-to-all-start.2
  43.2 6.4 %convolution_convert_fusion = bf16[2,2,4,32,4096]{4,2,3,1,0:T(4,128)(2,1)S(1)} fusion(bf16[4,32,4096,1,1]{2,1,0,4,3:T(8,128)(2,1)S(1)} %bitcast.149, f32[4,2,1,4]{0,3,2,1:T(4,128)S(1)} %get-tuple-element.37, f32[4,2,1,4]{0,3,2,1:T(4,128)S(1)} %get-tuple-element.36), kind=kOutput, calls=%fused_computation.15 | convolution fusion | flops 102760512 | bytes 5243136 | tf_op jit(solution)/shard_map/mgc,mlir->lirgc/dot_general | solution.py:108
  49.6 4.3 copy.70
  53.9 2.2 all-to-all-done.2
  56.2 5.0 %all-to-all-start.7 = ((bf16[2,2,4,32,4096]{4,3,1,0,2:T(8,128)(2,1)}), bf16[2,2,4,32,4096]{4,3,1,0,2:T(8,128)(2,1)}, u32[]{:S(2)}, u32[]{:S(2)}) async-start(bf16[2,2,4,32,4096]{4,3,1,0,2:T(8,128)(2,1)} %copy.70), calls=%async_computation.7 | async-start | bytes 8388608 | tf_op jit(solution)/shard_map/all_to_all | solution.py:119
  61.2 6.4 %convolution_convert_fusion.2 = bf16[2,2,4,32,4096]{4,2,3,1,0:T(4,128)(2,1)S(1)} fusion(bf16[4,32,4096,1,1]{2,1,0,4,3:T(8,128)(2,1)S(1)} %bitcast.145, f32[4,2,1,4]{0,3,2,1:T(4,128)S(1)} %get-tuple-element.37, f32[4,2,1,4]{0,3,2,1:T(4,128)S(1)} %get-tuple-element.36), kind=kOutput, calls=%fused_computation.17 | convolution fusion | flops 102760512 | bytes 5243136 | tf_op jit(solution)/shard_map/mgc,mlir->lirgc/dot_general | solution.py:108
  67.6 4.3 copy.54
  71.9 36.1 %all-to-all-done.7 = bf16[2,2,4,32,4096]{4,3,1,0,2:T(8,128)(2,1)} async-done(((bf16[2,2,4,32,4096]{4,3,1,0,2:T(8,128)(2,1)}), bf16[2,2,4,32,4096]{4,3,1,0,2:T(8,128)(2,1)}, u32[]{:S(2)}, u32[]{:S(2)}) %all-to-all-start.7) | async-done | bytes 4194336 | tf_op jit(solution)/shard_map/all_to_all | solution.py:119
  108.0 5.1 %all-to-all-start.1 = ((bf16[2,2,4,32,4096]{4,3,1,0,2:T(8,128)(2,1)}), bf16[2,2,4,32,4096]{4,3,1,0,2:T(8,128)(2,1)}, u32[]{:S(2)}, u32[]{:S(2)}) async-start(bf16[2,2,4,32,4096]{4,3,1,0,2:T(8,128)(2,1)} %copy.54), calls=%async_computation.1 | async-start | bytes 8388608 | tf_op jit(solution)/shard_map/all_to_all | solution.py:116
  113.1 6.4 %convolution_convert_fusion.1 = bf16[2,2,4,32,4096]{4,2,3,1,0:T(4,128)(2,1)S(1)} fusion(bf16[4,32,4096,1,1]{2,1,0,4,3:T(8,128)(2,1)S(1)} %bitcast.147, f32[4,2,1,4]{0,3,2,1:T(4,128)S(1)} %get-tuple-element.37, f32[4,2,1,4]{0,3,2,1:T(4,128)S(1)} %get-tuple-element.36), kind=kOutput, calls=%fused_computation.16 | convolution fusion | flops 102760512 | bytes 5243136 | tf_op jit(solution)/shard_map/mgc,mlir->lirgc/dot_general | solution.py:108
  119.5 4.3 copy.57
  123.8 36.2 %all-to-all-done.1 = bf16[2,2,4,32,4096]{4,3,1,0,2:T(8,128)(2,1)} async-done(((bf16[2,2,4,32,4096]{4,3,1,0,2:T(8,128)(2,1)}), bf16[2,2,4,32,4096]{4,3,1,0,2:T(8,128)(2,1)}, u32[]{:S(2)}, u32[]{:S(2)}) %all-to-all-start.1) | async-done | bytes 4194336 | tf_op jit(solution)/shard_map/all_to_all | solution.py:116
  160.0 5.3 %all-to-all-start.3 = ((bf16[2,2,4,32,4096]{4,3,1,0,2:T(8,128)(2,1)}), bf16[2,2,4,32,4096]{4,3,1,0,2:T(8,128)(2,1)}, u32[]{:S(2)}, u32[]{:S(2)}) async-start(bf16[2,2,4,32,4096]{4,3,1,0,2:T(8,128)(2,1)} %copy.57), calls=%async_computation.3 | async-start | bytes 8388608 | tf_op jit(solution)/shard_map/all_to_all | solution.py:113
  165.4 1.1 fusion.40
  166.6 2.5 copy.71
  169.1 2.5 copy.55
  171.5 5.6 %convolution_bitcast_fusion.2 = f32[2,2,128,4096]{3,2,1,0:T(8,128)} fusion(bf16[2,2,128,4096,1]{3,2,1,4,0:T(8,128)(2,1)S(1)} %bitcast.138, f32[2,1,128,2,128]{2,4,1,3,0:T(8,128)S(1)} %get-tuple-element.28, f32[2,1,128,2,128]{2,4,1,3,0:T(8,128)S(1)} %get-tuple-element.27), kind=kOutput, calls=%fused_computation.14 | convolution fusion | flops 6442582016 | bytes 13107200 | tf_op jit(solution)/shard_map/spjc,spjqb->sqbc/dot_general | solution.py:47
  177.1 5.7 %convolution_bitcast_fusion = f32[2,2,128,4096]{3,2,1,0:T(8,128)} fusion(bf16[2,2,128,4096,1]{3,2,1,4,0:T(8,128)(2,1)S(1)} %bitcast.136, f32[2,1,128,2,128]{2,4,1,3,0:T(8,128)S(1)} %get-tuple-element.28, f32[2,1,128,2,128]{2,4,1,3,0:T(8,128)S(1)} %get-tuple-element.27), kind=kOutput, calls=%fused_computation.12 | convolution fusion | flops 6442582016 | bytes 13107200 | tf_op jit(solution)/shard_map/spjc,spjqb->sqbc/dot_general | solution.py:47
  182.8 29.4 %all-to-all-done.3 = bf16[2,2,4,32,4096]{4,3,1,0,2:T(8,128)(2,1)} async-done(((bf16[2,2,4,32,4096]{4,3,1,0,2:T(8,128)(2,1)}), bf16[2,2,4,32,4096]{4,3,1,0,2:T(8,128)(2,1)}, u32[]{:S(2)}, u32[]{:S(2)}) %all-to-all-start.3) | async-done | bytes 4194336 | tf_op jit(solution)/shard_map/all_to_all | solution.py:113
  212.2 2.6 copy.58
  214.8 5.7 %convolution_bitcast_fusion.1 = f32[2,2,128,4096]{3,2,1,0:T(8,128)} fusion(bf16[2,2,128,4096,1]{3,2,1,4,0:T(8,128)(2,1)S(1)} %bitcast.137, f32[2,1,128,2,128]{2,4,1,3,0:T(8,128)S(1)} %get-tuple-element.28, f32[2,1,128,2,128]{2,4,1,3,0:T(8,128)S(1)} %get-tuple-element.27), kind=kOutput, calls=%fused_computation.13 | convolution fusion | flops 6442582016 | bytes 13107200 | tf_op jit(solution)/shard_map/spjc,spjqb->sqbc/dot_general | solution.py:47
  220.5 11.1 %multiply_add_fusion = (f32[2,1,128,4096]{3,2,1,0:T(8,128)S(1)}, f32[2,1,128,4096]{3,2,1,0:T(8,128)}, f32[2,1,128,4096]{3,2,1,0:T(8,128)}, f32[2,1,128,4096]{3,2,1,0:T(8,128)}) fusion(f32[2,2,128,4096]{3,2,1,0:T(8,128)} %convolution_bitcast_fusion, f32[2,2,128,4096]{3,2,1,0:T(8,128)} %convolution_bitcast_fusion.1, f32[2,2,128,4096]{3,2,1,0:T(8,128)S(1)} %bitcast.135), kind=kLoop, calls=%fused_computation.28 | loop fusion | flops 12582912 | bytes 41943040 | tf_op jit(solution)/shard_map/add | solution.py:70
  231.6 7.5 %maximum_bitcast_fusion = (f32[2,2,128,4096,1]{3,2,1,0,4:T(8,128)}, f32[2,2,128,4096,1]{3,2,1,0,4:T(8,128)S(1)}) fusion(f32[2,1,128,4096]{3,2,1,0:T(8,128)} %get-tuple-element.17, f32[2,1,128,4096]{3,2,1,0:T(8,128)} %get-tuple-element.18, f32[2,1,128,4096]{3,2,1,0:T(8,128)} %get-tuple-element.12, f32[2,1,128,4096]{3,2,1,0:T(8,128)S(1)} %get-tuple-element.11), kind=kLoop, calls=%fused_computation | loop fusion | flops 4194304 | bytes 33554432 | tf_op jit(solution)/shard_map/stack | solution.py:52
  239.2 8.0 %fusion = bf16[2,2,128,4096,1]{3,2,1,0,4:T(8,128)(2,1)S(1)} fusion(f32[2,2,128,4096,1]{3,2,1,0,4:T(8,128)S(1)} %get-tuple-element.39, f32[2,1,128,2,128]{2,4,3,0,1:T(8,128)S(1)} %get-tuple-element.26, f32[2,1,128,2,128]{2,4,3,0,1:T(8,128)S(1)} %get-tuple-element.25), kind=kOutput, calls=%fused_computation.4 | convolution fusion | flops 6442582016 | bytes 13107200 | tf_op jit(solution)/shard_map/sqbc,sqbpj->spjc/dot_general | solution.py:53
  247.7 6.4 %copy.80 = bf16[2,2,4,32,4096]{4,0,1,3,2:T(2,128)(2,1)} copy(bf16[2,2,4,32,4096]{4,3,2,0,1:T(8,128)(2,1)S(1)} %bitcast.140) | data formatting | bytes 8388608 | tf_op jit(solution)/shard_map/reshape | solution.py:133
  254.0 5.1 %all-to-all-start.10 = ((bf16[2,2,4,32,4096]{4,0,1,3,2:T(2,128)(2,1)}), bf16[2,2,4,32,4096]{4,0,1,3,2:T(2,128)(2,1)}, u32[]{:S(2)}, u32[]{:S(2)}) async-start(bf16[2,2,4,32,4096]{4,0,1,3,2:T(2,128)(2,1)} %copy.80), calls=%async_computation.10 | async-start | bytes 8388608 | tf_op jit(solution)/shard_map/all_to_all | solution.py:146
  259.1 6.5 %multiply_add_fusion.1 = (f32[2,1,128,4096]{3,2,1,0:T(8,128)S(1)}, f32[2,1,128,4096]{3,2,1,0:T(8,128)S(1)}) fusion(f32[2,2,128,4096]{3,2,1,0:T(8,128)} %convolution_bitcast_fusion, f32[2,2,128,4096]{3,2,1,0:T(8,128)} %convolution_bitcast_fusion.2), kind=kLoop, calls=%fused_computation.30 | loop fusion | flops 6291456 | bytes 25165824 | tf_op jit(solution)/shard_map/add | solution.py:67
  265.7 7.8 %fusion.2 = bf16[2,2,128,4096,1]{3,2,1,0,4:T(8,128)(2,1)S(1)} fusion(f32[2,1,128,2,128]{2,4,3,0,1:T(8,128)S(1)} %get-tuple-element.26, f32[2,1,128,2,128]{2,4,3,0,1:T(8,128)S(1)} %get-tuple-element.25, f32[2,1,128,4096]{3,2,1,0:T(8,128)S(1)} %get-tuple-element.14, f32[2,1,128,4096]{3,2,1,0:T(8,128)S(1)} %get-tuple-element.13), kind=kOutput, calls=%fused_computation.7 | convolution fusion | flops 6444679168 | bytes 13107200 | tf_op jit(solution)/shard_map/sqbc,sqbpj->spjc/dot_general | solution.py:53
  274.0 6.4 %copy.74 = bf16[2,2,4,32,4096]{4,0,1,3,2:T(2,128)(2,1)} copy(bf16[2,2,4,32,4096]{4,3,2,0,1:T(8,128)(2,1)S(1)} %bitcast.141) | data formatting | bytes 8388608 | tf_op jit(solution)/shard_map/reshape | solution.py:133
  280.4 25.6 %all-to-all-done.10 = bf16[2,2,4,32,4096]{4,0,1,3,2:T(2,128)(2,1)} async-done(((bf16[2,2,4,32,4096]{4,0,1,3,2:T(2,128)(2,1)}), bf16[2,2,4,32,4096]{4,0,1,3,2:T(2,128)(2,1)}, u32[]{:S(2)}, u32[]{:S(2)}) %all-to-all-start.10) | async-done | bytes 4194336 | tf_op jit(solution)/shard_map/all_to_all | solution.py:146
  306.0 5.1 %all-to-all-start.8 = ((bf16[2,2,4,32,4096]{4,0,1,3,2:T(2,128)(2,1)}), bf16[2,2,4,32,4096]{4,0,1,3,2:T(2,128)(2,1)}, u32[]{:S(2)}, u32[]{:S(2)}) async-start(bf16[2,2,4,32,4096]{4,0,1,3,2:T(2,128)(2,1)} %copy.74), calls=%async_computation.8 | async-start | bytes 8388608 | tf_op jit(solution)/shard_map/all_to_all | solution.py:145
  311.1 9.2 %fusion.4 = bf16[2,2,128,4096,1]{3,2,1,0,4:T(8,128)(2,1)S(1)} fusion(f32[2,2,128,4096,1]{3,2,1,0,4:T(8,128)} %get-tuple-element.38, f32[2,1,128,2,128]{2,4,3,0,1:T(8,128)S(1)} %get-tuple-element.26, f32[2,1,128,2,128]{2,4,3,0,1:T(8,128)S(1)} %get-tuple-element.25), kind=kOutput, calls=%fused_computation.10 | convolution fusion | flops 6442582016 | bytes 13107200 | tf_op jit(solution)/shard_map/sqbc,sqbpj->spjc/dot_general | solution.py:53
  321.4 0.6 pad_maximum_fusion
  322.0 6.4 %copy.65 = bf16[4,2,2,1,32,4096]{5,1,2,4,3,0:T(2,128)(2,1)} copy(bf16[4,2,2,1,32,4096]{5,4,2,1,3,0:T(8,128)(2,1)S(1)} %pad_maximum_fusion) | data formatting | bytes 8388608 | tf_op jit(solution)/shard_map/stack | solution.py:138
  328.4 29.6 %all-to-all-done.8 = bf16[2,2,4,32,4096]{4,0,1,3,2:T(2,128)(2,1)} async-done(((bf16[2,2,4,32,4096]{4,0,1,3,2:T(2,128)(2,1)}), bf16[2,2,4,32,4096]{4,0,1,3,2:T(2,128)(2,1)}, u32[]{:S(2)}, u32[]{:S(2)}) %all-to-all-start.8) | async-done | bytes 4194336 | tf_op jit(solution)/shard_map/all_to_all | solution.py:145
  358.0 5.4 %all-to-all-start.4 = ((bf16[4,2,2,1,32,4096]{5,1,2,4,3,0:T(2,128)(2,1)}), bf16[4,2,2,1,32,4096]{5,1,2,4,3,0:T(2,128)(2,1)}, u32[]{:S(2)}, u32[]{:S(2)}) async-start(bf16[4,2,2,1,32,4096]{5,1,2,4,3,0:T(2,128)(2,1)} %copy.65), calls=%async_computation.4 | async-start | bytes 8388608 | tf_op jit(solution)/shard_map/all_to_all | solution.py:137
  363.4 10.8 %fusion.7 = bf16[4,32,4096]{2,0,1:T(4,128)(2,1)S(1)} fusion(bf16[2,2,4,32,4096]{4,0,1,3,2:T(2,128)(2,1)} %all-to-all-done.8, f32[4,2,1,4]{0,3,2,1:T(4,128)S(1)} %get-tuple-element.37, f32[4,2,1,4]{0,3,2,1:T(4,128)S(1)} %get-tuple-element.36), kind=kOutput, calls=%fused_computation.22 | convolution fusion | flops 101187712 | bytes 5243136 | tf_op jit(solution)/shard_map/lirgc,mlir->mgc/dot_general | solution.py:151
  374.2 1.6 copy.77
  375.7 34.5 %all-to-all-done.4 = bf16[4,2,2,1,32,4096]{5,1,2,4,3,0:T(2,128)(2,1)} async-done(((bf16[4,2,2,1,32,4096]{5,1,2,4,3,0:T(2,128)(2,1)}), bf16[4,2,2,1,32,4096]{5,1,2,4,3,0:T(2,128)(2,1)}, u32[]{:S(2)}, u32[]{:S(2)}) %all-to-all-start.4) | async-done | bytes 4194336 | tf_op jit(solution)/shard_map/all_to_all | solution.py:137
  410.2 3.5 all-to-all-start.9
  413.8 10.8 %fusion.6 = bf16[4,32,4096]{2,0,1:T(4,128)(2,1)S(1)} fusion(bf16[4,2,2,1,32,4096]{5,1,2,4,3,0:T(2,128)(2,1)} %all-to-all-done.4, f32[4,2,1,4]{0,3,2,1:T(4,128)S(1)} %get-tuple-element.37, f32[4,2,1,4]{0,3,2,1:T(4,128)S(1)} %get-tuple-element.36), kind=kOutput, calls=%fused_computation.21 | convolution fusion | flops 101187712 | bytes 5243136 | tf_op jit(solution)/shard_map/lirgc,mlir->mgc/dot_general | solution.py:151
  424.6 1.6 copy.68
  426.1 0.7 all-to-all-done.9
  426.9 3.7 all-to-all-start.5
  430.6 10.8 %fusion.8 = bf16[4,32,4096]{2,0,1:T(4,128)(2,1)S(1)} fusion(bf16[2,2,4,32,4096]{4,0,1,3,2:T(2,128)(2,1)} %all-to-all-done.10, f32[4,2,1,4]{0,3,2,1:T(4,128)S(1)} %get-tuple-element.37, f32[4,2,1,4]{0,3,2,1:T(4,128)S(1)} %get-tuple-element.36), kind=kOutput, calls=%fused_computation.23 | convolution fusion | flops 101187712 | bytes 5243136 | tf_op jit(solution)/shard_map/lirgc,mlir->mgc/dot_general | solution.py:151
  441.4 1.6 copy.83
  443.0 0.6 all-to-all-done.5
  443.6 3.6 all-to-all-start.11
  447.2 5.5 %fusion.15 = (bf16[1,128,4096]{2,1,0:T(8,128)(2,1)}, bf16[1,128,4096]{2,1,0:T(8,128)(2,1)}, bf16[1,128,4096]{2,1,0:T(8,128)(2,1)}) fusion(bf16[1,128,4096]{2,1,0:T(8,128)(2,1)} %param.8, bf16[1,128,4096]{2,1,0:T(8,128)(2,1)} %get-tuple-element.9, f32[4096]{0:T(1024)S(1)} %bitcast.157, bf16[1,128,4096]{2,1,0:T(8,128)(2,1)} %param.9, ...), kind=kLoop, calls=%fused_computation.45 | loop fusion | flops 8912896 | bytes 10502144 | tf_op jit(solution)/shard_map/convert_element_type | solution.py:170
  452.7 1.3 collective-permute-start
  454.0 6.2 %all-to-all-done.11 = bf16[4,32,4096]{2,1,0:T(8,128)(2,1)S(1)} async-done(((bf16[4,32,4096]{2,1,0:T(8,128)(2,1)}), bf16[4,32,4096]{2,1,0:T(8,128)(2,1)S(1)}, u32[]{:S(2)}, u32[]{:S(2)}) %all-to-all-start.11) | async-done | bytes 1048608 | tf_op jit(solution)/shard_map/all_to_all | solution.py:158
  460.2 0.7 multiply_reduce_fusion
  461.0 15.3 %all-reduce = (bf16[1,4096]{1,0:T(2,128)(2,1)S(1)}, bf16[1,4096]{1,0:T(2,128)(2,1)S(1)}) all-reduce(bf16[1,4096]{1,0:T(2,128)(2,1)S(1)} %broadcast_in_dim.10, bf16[1,4096]{1,0:T(2,128)(2,1)S(1)} %broadcast_in_dim.12), channel_id=1, replica_groups=mesh['section'=8,'ctx'=4] {'ctx'}, use_global_device_ids=true, to_apply=%region_1.2 | all-reduce | flops 8192 | bytes 32768 | tf_op jit(solution)/shard_map/psum | solution.py:176
  476.3 0.6 broadcast_in_dim.11
  476.9 0.6 broadcast_in_dim.13
  477.8 1.4 fusion.21
  479.1 1.0 copy.166
  (37 shorter events, 2.6 us)
Async XLA Ops:
  0.6 8.7 %copy-start.3 = (bf16[1,128,4096]{2,1,0:T(8,128)(2,1)S(1)}, bf16[1,128,4096]{2,1,0:T(8,128)(2,1)}, u32[]{:S(2)}) copy-start(bf16[1,128,4096]{2,1,0:T(8,128)(2,1)} %param.13) | copy-start | bytes 3145732
  0.6 8.7 %copy-start.2 = (bf16[1,128,4096]{2,1,0:T(8,128)(2,1)S(1)}, bf16[1,128,4096]{2,1,0:T(8,128)(2,1)}, u32[]{:S(2)}) copy-start(bf16[1,128,4096]{2,1,0:T(8,128)(2,1)} %param.8) | copy-start | bytes 3145732
  4.2 18.8 %all-to-all-start = ((bf16[4,32,4096]{2,1,0:T(8,128)(2,1)}), bf16[4,32,4096]{2,1,0:T(8,128)(2,1)S(1)}, u32[]{:S(2)}, u32[]{:S(2)}) async-start(bf16[4,32,4096]{2,1,0:T(8,128)(2,1)} %fusion.22), calls=%async_computation | async-start | bytes 2097152 | tf_op jit(solution)/shard_map/all_to_all | solution.py:100
  23.0 16.6 %all-to-all-start.6 = ((bf16[4,32,4096]{2,1,0:T(8,128)(2,1)}), bf16[4,32,4096]{2,1,0:T(8,128)(2,1)S(1)}, u32[]{:S(2)}, u32[]{:S(2)}) async-start(bf16[4,32,4096]{2,1,0:T(8,128)(2,1)} %bitcast.38), calls=%async_computation.6 | async-start | bytes 2097152 | tf_op jit(solution)/shard_map/all_to_all | solution.py:103
  39.6 16.6 %all-to-all-start.2 = ((bf16[4,32,4096]{2,1,0:T(8,128)(2,1)}), bf16[4,32,4096]{2,1,0:T(8,128)(2,1)S(1)}, u32[]{:S(2)}, u32[]{:S(2)}) async-start(bf16[4,32,4096]{2,1,0:T(8,128)(2,1)} %bitcast.17), calls=%async_computation.2 | async-start | bytes 2097152 | tf_op jit(solution)/shard_map/all_to_all | solution.py:97
  56.2 51.9 %all-to-all-start.7 = ((bf16[2,2,4,32,4096]{4,3,1,0,2:T(8,128)(2,1)}), bf16[2,2,4,32,4096]{4,3,1,0,2:T(8,128)(2,1)}, u32[]{:S(2)}, u32[]{:S(2)}) async-start(bf16[2,2,4,32,4096]{4,3,1,0,2:T(8,128)(2,1)} %copy.70), calls=%async_computation.7 | async-start | bytes 8388608 | tf_op jit(solution)/shard_map/all_to_all | solution.py:119
  108.0 52.0 %all-to-all-start.1 = ((bf16[2,2,4,32,4096]{4,3,1,0,2:T(8,128)(2,1)}), bf16[2,2,4,32,4096]{4,3,1,0,2:T(8,128)(2,1)}, u32[]{:S(2)}, u32[]{:S(2)}) async-start(bf16[2,2,4,32,4096]{4,3,1,0,2:T(8,128)(2,1)} %copy.54), calls=%async_computation.1 | async-start | bytes 8388608 | tf_op jit(solution)/shard_map/all_to_all | solution.py:116
  160.0 52.2 %all-to-all-start.3 = ((bf16[2,2,4,32,4096]{4,3,1,0,2:T(8,128)(2,1)}), bf16[2,2,4,32,4096]{4,3,1,0,2:T(8,128)(2,1)}, u32[]{:S(2)}, u32[]{:S(2)}) async-start(bf16[2,2,4,32,4096]{4,3,1,0,2:T(8,128)(2,1)} %copy.57), calls=%async_computation.3 | async-start | bytes 8388608 | tf_op jit(solution)/shard_map/all_to_all | solution.py:113
  212.2 8.3 %slice-start = ((s8[8388608]{0:T(1024)(128)(4,1)}), s8[4194304]{0:T(1024)(128)(4,1)S(1)}, s32[]{:S(2)}) async-start(s8[8388608]{0:T(1024)(128)(4,1)} %bitcast.134), calls=%async_computation.12 | async-start | bytes 8388608
  214.8 5.7 %slice-start.1 = ((s8[8388608]{0:T(1024)(128)(4,1)}), s8[4194304]{0:T(1024)(128)(4,1)S(1)}, s32[]{:S(2)}) async-start(s8[8388608]{0:T(1024)(128)(4,1)} %bitcast.134), calls=%async_computation.13 | async-start | bytes 8388608
  254.0 52.0 %all-to-all-start.10 = ((bf16[2,2,4,32,4096]{4,0,1,3,2:T(2,128)(2,1)}), bf16[2,2,4,32,4096]{4,0,1,3,2:T(2,128)(2,1)}, u32[]{:S(2)}, u32[]{:S(2)}) async-start(bf16[2,2,4,32,4096]{4,0,1,3,2:T(2,128)(2,1)} %copy.80), calls=%async_computation.10 | async-start | bytes 8388608 | tf_op jit(solution)/shard_map/all_to_all | solution.py:146
  306.0 52.0 %all-to-all-start.8 = ((bf16[2,2,4,32,4096]{4,0,1,3,2:T(2,128)(2,1)}), bf16[2,2,4,32,4096]{4,0,1,3,2:T(2,128)(2,1)}, u32[]{:S(2)}, u32[]{:S(2)}) async-start(bf16[2,2,4,32,4096]{4,0,1,3,2:T(2,128)(2,1)} %copy.74), calls=%async_computation.8 | async-start | bytes 8388608 | tf_op jit(solution)/shard_map/all_to_all | solution.py:145
  358.0 52.3 %all-to-all-start.4 = ((bf16[4,2,2,1,32,4096]{5,1,2,4,3,0:T(2,128)(2,1)}), bf16[4,2,2,1,32,4096]{5,1,2,4,3,0:T(2,128)(2,1)}, u32[]{:S(2)}, u32[]{:S(2)}) async-start(bf16[4,2,2,1,32,4096]{5,1,2,4,3,0:T(2,128)(2,1)} %copy.65), calls=%async_computation.4 | async-start | bytes 8388608 | tf_op jit(solution)/shard_map/all_to_all | solution.py:137
  410.2 16.6 %all-to-all-start.9 = ((bf16[4,32,4096]{2,1,0:T(8,128)(2,1)}), bf16[4,32,4096]{2,1,0:T(8,128)(2,1)S(1)}, u32[]{:S(2)}, u32[]{:S(2)}) async-start(bf16[4,32,4096]{2,1,0:T(8,128)(2,1)} %copy.77), calls=%async_computation.9 | async-start | bytes 2097152 | tf_op jit(solution)/shard_map/all_to_all | solution.py:157
  426.9 16.7 %all-to-all-start.5 = ((bf16[4,32,4096]{2,1,0:T(8,128)(2,1)}), bf16[4,32,4096]{2,1,0:T(8,128)(2,1)S(1)}, u32[]{:S(2)}, u32[]{:S(2)}) async-start(bf16[4,32,4096]{2,1,0:T(8,128)(2,1)} %copy.68), calls=%async_computation.5 | async-start | bytes 2097152 | tf_op jit(solution)/shard_map/all_to_all | solution.py:156
  441.4 5.7 %copy-start.4 = (f32[1,4096]{1,0:T(1,128)S(1)}, f32[1,4096]{1,0:T(1,128)}, u32[]{:S(2)}) copy-start(f32[1,4096]{1,0:T(1,128)} %param.12) | copy-start | bytes 49156
  443.6 3.6 copy-start.1
  443.6 16.6 %all-to-all-start.11 = ((bf16[4,32,4096]{2,1,0:T(8,128)(2,1)}), bf16[4,32,4096]{2,1,0:T(8,128)(2,1)S(1)}, u32[]{:S(2)}, u32[]{:S(2)}) async-start(bf16[4,32,4096]{2,1,0:T(8,128)(2,1)} %copy.83), calls=%async_computation.11 | async-start | bytes 2097152 | tf_op jit(solution)/shard_map/all_to_all | solution.py:158
  447.2 13.0 %copy-start = (bf16[1,128,4096]{2,1,0:T(8,128)(2,1)S(1)}, bf16[1,128,4096]{2,1,0:T(8,128)(2,1)}, u32[]{:S(2)}) copy-start(bf16[1,128,4096]{2,1,0:T(8,128)(2,1)} %param.10) | copy-start | bytes 3145732
  452.7 26.4 %collective-permute-start = (bf16[1,128,4096]{2,1,0:T(8,128)(2,1)}, bf16[1,128,4096]{2,1,0:T(8,128)(2,1)S(1)}, u32[]{:S(2)}, u32[]{:S(2)}) collective-permute-start(bf16[1,128,4096]{2,1,0:T(8,128)(2,1)} %get-tuple-element.23), channel_id=1, source_target_pairs={{4,0},{8,4},{12,8},{16,12},{20,16},{24,20},{28,24},{5,1},{9,5},{13... | collective-permute-start | bytes 3145736 | tf_op jit(solution)/shard_map/ppermute | solution.py:13
